TPU v7x, 32 devices: a whole 2x2x4 slice. The times are simulated.
32 devices in a mesh: in: 4 (over z), out: 8 (over y, x, core).
Axes of the slice: x: 2, y: 2, z: 4, core: 2. Of those that a mesh axis runs over, the one named last changes fastest.
Arguments:
- activations: bfloat16 [512, 5120], P('out', 'in'), may hold values from -6 to 6
- act_basis: bfloat16 [5120, 5120], P(None, 'in'), may hold values from -0.078125 to 0.078125
- gradients: bfloat16 [512, 20480], P('out', 'in'), may hold values from -0.59765625 to 0.59765625
- grad_basis: bfloat16 [20480, 20480], P('in', 'out'), may hold values from -0.0390625 to 0.0390625
- lengths: int32 [4], replicated, may hold values from 1 to 128, 384 in all
- sample_weights: int32 [4], replicated, may hold values from 1 to 4
Outputs:
- eigenvalues: float32 [20480, 5120], P('out', 'in')
Inputs may be any that keep to these rules, and one draw needn't show every extreme that they name: Some sequence is full, every sequence has at least one valid token, and the lengths sum to 384.
All inputs are finite; a program needn't handle non-finite values.
Results may differ from a plain program's by a relative error of at most 0.0031.
Values may be sent and summed in bfloat16 or wider, within the bound.
No kernel may reach another device: no remote copies, remote signals or barrier semaphores. Data moves between devices by JAX's collectives and lax.ppermute only.
A program may use at most 128 MiB of HBM per device.

v0:
```python
import jax
import jax.numpy as jnp
from jax import lax
from jax.sharding import PartitionSpec as P


def local(activations, act_basis, gradients, grad_basis, lengths, sample_weights):
    width_in = act_basis.shape[1]
    local_rot = jnp.dot(
        lax.all_gather(activations, "in", axis=1, tiled=True),
        act_basis,
        preferred_element_type=jnp.float32,
    ).astype(jnp.bfloat16)
    rot_act = lax.all_gather(local_rot, "out", axis=0, tiled=True)
    seq_count = lengths.shape[0]
    slot_count = rot_act.shape[0] // seq_count
    positions = jnp.arange(slot_count, dtype=jnp.int32)
    valid_flags = positions[None, :] < lengths[:, None]
    valid = valid_flags.astype(jnp.bfloat16)
    partial_rot = jnp.dot(
        lax.all_gather(gradients, "out", axis=0, tiled=True),
        grad_basis,
        preferred_element_type=jnp.float32,
    )
    rot_rows = lax.psum(partial_rot, "in").astype(jnp.bfloat16)
    act_seq = rot_act.reshape(seq_count, slot_count, width_in)
    grad_seq = rot_rows.reshape(seq_count, slot_count, rot_rows.shape[1]) * valid[:, :, None]
    weights = sample_weights.astype(jnp.float32)

    def accumulate(total, item):
        grad_one, act_one, weight = item
        block = lax.dot_general(
            grad_one, act_one, (((0,), (0,)), ((), ())), preferred_element_type=jnp.float32
        )
        return (total + weight * block * block, None)

    start_total = jnp.zeros((rot_rows.shape[1], width_in), jnp.float32)
    total, unused = lax.scan(accumulate, start_total, (grad_seq, act_seq, weights))
    return total / jnp.sum(weights)


def solution(mesh):
    in_specs = (P("out", "in"), P(None, "in"), P("out", "in"), P("in", "out"), P(), P())
    out_specs = P("out", "in")
    return jax.shard_map(local, mesh=mesh, in_specs=in_specs, out_specs=out_specs, check_vma=False)
```

profile of v0, /device:TPU:0, one launch (start us, length us, event | category | flops | bytes accessed | tf_op | source)
XLA Modules:
  0.0 314.9 jit_solution(15778276582313871719)
XLA Ops:
  6.5 0.0 copy-start
  6.5 0.0 copy-start.1
  6.5 0.0 all-gather.3.cloned.1.call-start
  6.5 0.7 all-gather.3.cloned.1.call-update
  7.3 0.0 all-gather.5.cloned.1.call-start
  7.3 19.9 %all_gather.10 = bf16[64,5120]{1,0:T(8,128)(2,1)S(1)} all-gather(bf16[64,1280]{1,0:T(8,128)(2,1)} %param.8), channel_id=1, replica_groups=mesh['in'=4,'out'=8] {'in'}, dimensions={1}, use_global_device_ids=true | all-gather | bytes 819200 | tf_op jit(solution)/shard_map/all_gather | solution.py:10
  27.2 7.7 %convolution_convert_fusion = bf16[64,1280]{1,0:T(8,128)(2,1)} fusion(bf16[64,5120]{1,0:T(8,128)(2,1)S(1)} %all_gather.10, bf16[5120,1280]{1,0:T(8,128)(2,1)} %param.9), kind=kOutput, calls=%fused_computation.8 | convolution fusion | flops 838942720 | bytes 13926400 | tf_op jit(solution)/shard_map/dot_general | solution.py:9
  35.0 0.0 all-gather.5.cloned.1.call-update
  35.0 0.0 copy-done
  35.0 0.7 convert_reduce_fusion
  35.7 0.0 copy-done.1
  35.7 0.1 fusion.6
  35.8 17.2 %all-gather.3.cloned.1.call-done = bf16[512,5120]{1,0:T(8,128)(2,1)} async-done(((bf16[64,5120]{1,0:T(8,128)(2,1)}), bf16[512,5120]{1,0:T(8,128)(2,1)}) %all-gather.3.cloned.1.call-update) | async-done | bytes 5242896 | tf_op jit(solution)/shard_map/all_gather | solution.py:21
  53.0 21.6 %fusion.7 = f32[512,2560]{1,0:T(8,128)} fusion(bf16[512,5120]{1,0:T(8,128)(2,1)} %all-gather.3.cloned.1.call-done, bf16[5120,2560]{1,0:T(8,128)(2,1)} %param.11), kind=kOutput, calls=%fused_computation.13 | convolution fusion | flops 13421772800 | bytes 36700160 | tf_op jit(solution)/shard_map/dot_general | solution.py:20
  74.6 181.7 %all-reduce.1 = bf16[512,2560]{1,0:T(8,128)(2,1)} all-reduce(f32[512,2560]{1,0:T(8,128)} %fusion.7), channel_id=1, replica_groups=mesh['in'=4,'out'=8] {'in'}, use_global_device_ids=true, to_apply=%region_0.0 | all-reduce | flops 1310720 | bytes 7864320 | tf_op jit(solution)/shard_map/psum | solution.py:25
  256.3 2.0 broadcast_multiply_fusion
  258.3 0.0 all-gather.5.cloned.1.call-done
  258.3 38.5 %while.11 = (s32[]{:T(128)}, f32[2560,1280]{1,0:T(8,128)}, f32[4]{0:T(128)S(1)}, bf16[4,128,2560]{2,1,0:T(8,128)(2,1)S(1)}, bf16[4,128,1280]{2,1,0:T(8,128)(2,1)}, /*index=5*/s32[]{:T(128)}, s32[]{:T(128)}) while((s32[]{:T(128)}, f32[2560,1280]{1,0:T(8,128)}, f32[4]{0:T(128)S(1)}, bf16[4,128,2560]{2,1,0:T(8,128)(2,1)S(1)}, ...), condition=%wide.region_2.3_spmd.clone, body=%wide.region_1.2_spmd.clone.sunk | while | flops 851968000 | bytes 27199072 | solution.py:38
  258.3 0.6 dynamic_slice.28
  258.9 7.6 %fusion.17 = f32[2560,1280]{1,0:T(8,128)} fusion(f32[2560,1280]{1,0:T(8,128)} %get-tuple-element.100, f32[]{:T(128)} %bitcast.18, pred[]{:T(512)S(6)} %compare.3, bf16[4,128,2560]{2,1,0:T(8,128)(2,1)S(1)} %get-tuple-element.109, s32[]{:T(128)} %get-tuple-element.99, bf16[4,128,1280]{2,1,0:T(8,128)(2,1)} %get-tuple-element.110), kind=kOutput, calls=%fused_computation.1.clone.1 | convolution fusion | flops 851968000 | bytes 27198976 | tf_op jit(solution)/shard_map/while/body/eval_jaxpr/dot_general | solution.py:32
  266.6 0.6 dynamic_slice.28
  267.2 9.5 %fusion.17 = f32[2560,1280]{1,0:T(8,128)} fusion(f32[2560,1280]{1,0:T(8,128)} %get-tuple-element.100, f32[]{:T(128)} %bitcast.18, pred[]{:T(512)S(6)} %compare.3, bf16[4,128,2560]{2,1,0:T(8,128)(2,1)S(1)} %get-tuple-element.109, s32[]{:T(128)} %get-tuple-element.99, bf16[4,128,1280]{2,1,0:T(8,128)(2,1)} %get-tuple-element.110), kind=kOutput, calls=%fused_computation.1.clone.1 | convolution fusion | flops 851968000 | bytes 27198976 | tf_op jit(solution)/shard_map/while/body/eval_jaxpr/dot_general | solution.py:32
  276.6 0.6 dynamic_slice.28
  277.2 9.5 %fusion.17 = f32[2560,1280]{1,0:T(8,128)} fusion(f32[2560,1280]{1,0:T(8,128)} %get-tuple-element.100, f32[]{:T(128)} %bitcast.18, pred[]{:T(512)S(6)} %compare.3, bf16[4,128,2560]{2,1,0:T(8,128)(2,1)S(1)} %get-tuple-element.109, s32[]{:T(128)} %get-tuple-element.99, bf16[4,128,1280]{2,1,0:T(8,128)(2,1)} %get-tuple-element.110), kind=kOutput, calls=%fused_computation.1.clone.1 | convolution fusion | flops 851968000 | bytes 27198976 | tf_op jit(solution)/shard_map/while/body/eval_jaxpr/dot_general | solution.py:32
  286.7 0.6 dynamic_slice.28
  287.3 9.5 %fusion.17 = f32[2560,1280]{1,0:T(8,128)} fusion(f32[2560,1280]{1,0:T(8,128)} %get-tuple-element.100, f32[]{:T(128)} %bitcast.18, pred[]{:T(512)S(6)} %compare.3, bf16[4,128,2560]{2,1,0:T(8,128)(2,1)S(1)} %get-tuple-element.109, s32[]{:T(128)} %get-tuple-element.99, bf16[4,128,1280]{2,1,0:T(8,128)(2,1)} %get-tuple-element.110), kind=kOutput, calls=%fused_computation.1.clone.1 | convolution fusion | flops 851968000 | bytes 27198976 | tf_op jit(solution)/shard_map/while/body/eval_jaxpr/dot_general | solution.py:32
  296.8 11.2 %broadcast_divide_fusion = f32[2560,1280]{1,0:T(8,128)} fusion(f32[2560,1280]{1,0:T(8,128)} %get-tuple-element.32, f32[]{:T(128)} %convert_reduce_fusion), kind=kLoop, calls=%fused_computation.7 | loop fusion | flops 3276800 | bytes 26214404 | tf_op jit(solution)/shard_map/div | solution.py:39
  (2 shorter events, 0.0 us)
Async XLA Ops:
  6.5 28.5 %copy-start = (s32[4]{0:T(128)S(1)}, s32[4]{0:T(128)}, u32[]{:S(2)}) copy-start(s32[4]{0:T(128)} %param.13) | copy-start | bytes 52
  6.5 29.2 %copy-start.1 = (s32[4]{0:T(128)S(1)}, s32[4]{0:T(128)}, u32[]{:S(2)}) copy-start(s32[4]{0:T(128)} %param.12) | copy-start | bytes 52
  6.5 46.4 %all-gather.3.cloned.1.call-start = ((), (), s32[]{:S(2)}) async-start(), calls=%async_computation | async-start | bytes 5898240 | tf_op jit(solution)/shard_map/all_gather | solution.py:21
  7.3 251.0 %all-gather.5.cloned.1.call-start = ((), (), s32[]{:S(2)}) async-start(), calls=%async_computation.1 | async-start | bytes 1474560 | tf_op jit(solution)/shard_map/all_gather | solution.py:14
Sparse Core Ops, SparseCore 0:
  9.2 43.6 all-gather.2
  54.8 24.4 all-gather.4
where the time goes:
time: 315 us
  blocking collectives  202 us (64%)
  matrix products  65.4 us (21%)
  waiting for transfers between devices  17.9 us (6%)
  other arithmetic  13.9 us (4%)
  between operations  13.4 us (4%)
    psum x1, blocking collectives, local(): rot_rows = lax.psum(partial_rot, 'in').astype(jnp.bfloat16)  182 us
    dot_general x4, matrix products, accumulate(): lax.dot_general(grad_one, act_one, (((0,), (0,)), ((), ())), preferred_el...  36.1 us
    dot_general x1, matrix products, local(): jnp.dot(lax.all_gather(gradients, 'out', axis=0, tiled=True), grad_basis,...  21.6 us
    all_gather x1, blocking collectives, local(): lax.all_gather(activations, 'in', axis=1, tiled=True)  19.9 us
    all_gather x1, waiting for transfers between devices, local(): lax.all_gather(gradients, 'out', axis=0, tiled=True)  17.2 us
    div x1, other arithmetic, local(): return total / jnp.sum(weights)  11.2 us
    dot_general x1, matrix products, local(): jnp.dot(lax.all_gather(activations, 'in', axis=1, tiled=True), act_basis,...  7.74 us
  transfers between devices with their start and end apart: 2, of which 1 were waited for; matrix products, arithmetic and copies ran while one was open for 10% of the time, Pallas kernels for 0%

commit v1 on v0

v1 whole, which is shorter than its diff:
```python
import jax
import jax.numpy as jnp
from jax import lax
from jax.experimental import pallas as pl
from jax.experimental.pallas import tpu as pltpu
from jax.sharding import PartitionSpec as P

CHUNKS = 2
GROUPS = 5
LAG = 2


def generic(activations, act_basis, gradients, grad_basis, lengths, sample_weights):
    width_in = act_basis.shape[1]
    local_rot = jnp.dot(
        lax.all_gather(activations, "in", axis=1, tiled=True), act_basis, preferred_element_type=jnp.float32
    ).astype(jnp.bfloat16)
    rot_act = lax.all_gather(local_rot, "out", axis=0, tiled=True)
    seq_count = lengths.shape[0]
    slot_count = rot_act.shape[0] // seq_count
    positions = jnp.arange(slot_count, dtype=jnp.int32)
    valid = (positions[None, :] < lengths[:, None]).astype(jnp.bfloat16)
    partial_rot = jnp.dot(
        lax.all_gather(gradients, "out", axis=0, tiled=True), grad_basis, preferred_element_type=jnp.float32
    )
    rot_rows = lax.psum(partial_rot, "in").astype(jnp.bfloat16)
    act_seq = rot_act.reshape(seq_count, slot_count, width_in)
    grad_seq = rot_rows.reshape(seq_count, slot_count, rot_rows.shape[1]) * valid[:, :, None]
    weights = sample_weights.astype(jnp.float32)

    def accumulate(total, item):
        grad_one, act_one, weight = item
        block = lax.dot_general(
            grad_one, act_one, (((0,), (0,)), ((), ())), preferred_element_type=jnp.float32
        )
        return (total + weight * block * block, None)

    start_total = jnp.zeros((rot_rows.shape[1], width_in), jnp.float32)
    total, unused = lax.scan(accumulate, start_total, (grad_seq, act_seq, weights))
    return total / jnp.sum(weights)


def squares_kernel(place_ref, weight_ref, pick_ref, s_ref, even_ref, odd_ref, out_ref):
    count = weight_ref.shape[0]
    half = even_ref.shape[0] // count
    chip = place_ref[0] // 2
    weights = [weight_ref[n].astype(jnp.float32) for n in range(count)]
    whole = weights[0]
    for n in range(1, count):
        whole = whole + weights[n]
    s = jnp.concatenate([ref[...] for ref in s_ref], axis=0)
    total = None
    for n in range(count):
        pick = pick_ref[2 * half * n:2 * half * (n + 1), :]
        rows = jnp.dot(pick, s, preferred_element_type=jnp.float32).astype(jnp.bfloat16)
        acts = jnp.concatenate(
            [even_ref[half * n:half * (n + 1), :], odd_ref[half * n:half * (n + 1), :]], axis=0
        )
        example = lax.dot_general(rows, acts, (((0,), (0,)), ((), ())), preferred_element_type=jnp.float32)
        scale = weight_ref[lax.bitwise_xor(chip, n)].astype(jnp.float32) / whole
        term = (scale * example) * example
        total = term if total is None else total + term
    out_ref[...] = total


def squares(place, sample_weights, pick, parts, even, odd, out, group, height):
    cols = parts[0].shape[1]
    width = even.shape[1]

    def body(place_ref, weight_ref, pick_ref, *rest):
        s_refs, rest = rest[:len(parts)], rest[len(parts):]
        squares_kernel(place_ref, weight_ref, pick_ref, s_refs, rest[0], rest[1], rest[-1])

    tail, aliases = [], {}
    specs = [
        pl.BlockSpec(memory_space=pltpu.SMEM),
        pl.BlockSpec(memory_space=pltpu.SMEM),
        pl.BlockSpec(pick.shape, lambda i: (0, 0)),
    ]
    specs += [pl.BlockSpec(part.shape, lambda i: (0, 0)) for part in parts]
    specs += [pl.BlockSpec(even.shape, lambda i: (0, 0)), pl.BlockSpec(odd.shape, lambda i: (0, 0))]
    if out is not None:
        tail = [out]
        aliases = {len(specs): 0}
        specs.append(pl.BlockSpec(memory_space=pl.ANY))
    return pl.pallas_call(
        body,
        grid=(1,),
        in_specs=specs,
        out_specs=pl.BlockSpec((cols, width), lambda i: (group, 0)),
        out_shape=jax.ShapeDtypeStruct((height, width), jnp.float32),
        input_output_aliases=aliases,
        compiler_params=pltpu.CompilerParams(vmem_limit_bytes=26 << 20),
        cost_estimate=pl.CostEstimate(
            flops=4 * cols * width * pick.shape[0], bytes_accessed=4 * cols * width + 4 * even.size, transcendentals=0
        ),
    )(place, sample_weights, pick, *parts, even, odd, *tail)


def line(activations, act_basis, gradients, grad_basis, lengths, sample_weights):
    bf16, f16 = jnp.bfloat16, jnp.float16
    slots, wide = gradients.shape
    seqs = lengths.shape[0]
    z = lax.axis_index("in")
    o = lax.axis_index("out")

    def swap(x, bit):
        return lax.ppermute(x, "out", [(i, i ^ bit) for i in range(2 * seqs)])

    step = slots // CHUNKS
    mid = wide // 2
    chunks = []
    for k in range(CHUNKS):
        rows = gradients[k * step:(k + 1) * step]
        parts = []
        for cols, bits in ((rows[:, :mid], (2, 4)), (rows[:, mid:], (4, 2))):
            for bit in bits:
                cols = jnp.concatenate([cols, swap(cols, bit)], axis=0)
            parts.append((cols, swap(cols, 1)))
        chunks.append(parts)

    shifted = [activations] + [
        lax.ppermute(activations, "in", [(i, (i + d) % 4) for i in range(4)]) for d in (1, 2, 3)
    ]
    block = activations.shape[1]

    n_of = jnp.arange(seqs, dtype=jnp.int32)
    q_at = jnp.arange(CHUNKS, dtype=jnp.int32)[:, None, None]
    b_at = jnp.arange(2, dtype=jnp.int32)[None, None, :]
    counts = jnp.clip(lengths[None, :, None] - b_at * slots - q_at * step, 0, step)
    counts = counts.reshape(-1)
    label = jnp.arange(counts.shape[0], dtype=jnp.int32)

    def packed_index(q, dev, r):
        mine = (q * seqs + dev // 2) * 2 + dev % 2
        before = jnp.sum(jnp.where(label[None, :] < mine[:, None], counts[None, :], 0), axis=1)
        have = jnp.sum(jnp.where(label[None, :] == mine[:, None], counts[None, :], 0), axis=1)
        return jnp.where(r < have, before + r, -1)

    total_rows = slots * 2 * seqs * 3 // 4
    packed_rows = total_rows // CHUNKS

    def slot_index(order):
        out = []
        pos = jnp.arange(len(order) * step, dtype=jnp.int32)
        dev = lax.bitwise_xor(o, sum(jnp.where(pos // step == i, p, 0) for i, p in enumerate(order)).astype(jnp.int32))
        for q in range(CHUNKS):
            out.append(packed_index(jnp.int32(q), dev, pos % step))
        return out

    first = ((0, 2, 4, 6), (1, 3, 5, 7))
    second = ((0, 4, 2, 6), (1, 5, 3, 7))

    def one_hot(index, start):
        return (index[None, :] == start + jnp.arange(packed_rows, dtype=jnp.int32)[:, None]).astype(bf16)

    packed = []
    for k in range(CHUNKS):
        halves = []
        for side, orders in enumerate((first, second)):
            hots, rows = [], []
            for half in (0, 1):
                index = slot_index(orders[half])
                for q in range(k + 1):
                    hots.append(one_hot(index[q], k * packed_rows))
                    rows.append(chunks[q][side][half])
            halves.append(
                jnp.dot(
                    jnp.concatenate(hots, axis=1), jnp.concatenate(rows, axis=0), preferred_element_type=jnp.float32
                ).astype(bf16)
            )
        packed.append(jnp.concatenate(halves, axis=1))

    height = grad_basis.shape[1]
    cut = height // GROUPS
    tiles = CHUNKS * GROUPS
    own = []
    for k in range(CHUNKS):
        for g in range(GROUPS):
            own.append(
                jnp.dot(
                    packed[k], grad_basis[:, g * cut:(g + 1) * cut], preferred_element_type=jnp.float32
                ).astype(f16)
            )

    outer = (z == 0) | (z == 3)
    inward, outward, middle = [(0, 1), (3, 2)], [(1, 0), (2, 3)], [(1, 2), (2, 1)]
    ends, mids = {}, {}
    for s in range(tiles + 2 * LAG):
        back = s - 2 * LAG
        if back < 0:
            operand, pairs = own[s], inward
        else:
            operand, pairs = own[back] + mids[back], outward
            if s < tiles:
                operand, pairs = jnp.where(outer, own[s], operand), inward + outward
        ends[s] = lax.ppermute(operand, "in", pairs)
        c = s - LAG
        if 0 <= c < tiles:
            mids[c] = lax.ppermute(own[c] + ends[c], "in", middle)
    f32 = jnp.float32
    sums = [
        (
            own[c].astype(f32)
            + jnp.where(outer, ends[c + 2 * LAG], ends[c]).astype(f32)
            + mids[c].astype(f32)
        ).astype(bf16)
        for c in range(tiles)
    ]

    acts = jnp.zeros((activations.shape[0], act_basis.shape[0]), bf16)
    for d, piece in enumerate(shifted):
        acts = lax.dynamic_update_slice(acts, piece, (0, lax.rem(z + 4 - d, 4) * block))
    rot = jnp.dot(acts, act_basis, preferred_element_type=f32).astype(bf16)
    even = jnp.concatenate([rot, swap(rot, 2)], axis=0)
    even = jnp.concatenate([even, swap(even, 4)], axis=0)
    odd = swap(even, 1)

    pos = jnp.arange(2 * seqs * slots, dtype=jnp.int32)
    at = pos // slots
    row = pos % slots
    index = packed_index(row // step, lax.bitwise_xor(o, at), row % step)
    pick = (index[:, None] == jnp.arange(total_rows, dtype=jnp.int32)[None, :]).astype(bf16)

    place = o.reshape(1)
    out = None
    for g in range(GROUPS):
        parts = [sums[k * GROUPS + g] for k in range(CHUNKS)]
        out = squares(place, sample_weights, pick, parts, even, odd, out, g, height)
    return out


def solution(mesh):
    in_specs = (P("out", "in"), P(None, "in"), P("out", "in"), P("in", "out"), P(), P())
    out_specs = P("out", "in")
    body = line if mesh.shape["in"] == 4 and mesh.shape["out"] == 8 else generic
    return jax.shard_map(body, mesh=mesh, in_specs=in_specs, out_specs=out_specs, check_vma=False)
```

time: 315 us -> 185 us (0.59)
  blocking collectives: 202 us -> 0 us
  starting transfers between devices: 0.04 us -> 67 us
  matrix products: 65.4 us -> 28.1 us
  waiting for transfers between devices: 17.9 us -> 47.8 us
  Pallas kernels: 0 us -> 22.5 us
  between operations: 13.4 us -> 0.91 us
  local copies, waits for them, and re-layouts: 2.41 us -> 10.2 us
  other arithmetic: 13.9 us -> 7.66 us
    psum x1 -> x0, blocking collectives: 182 us -> none  [local(): rot_rows = lax.psum(partial_rot, 'in').astype(jnp.bfloat16)]
    ppermute x0 -> x42, starting transfers between devices: none -> 67 us  [the longest x14 41.7 us: line(): ends[s] = lax.ppermute(operand, 'in', pairs)]
    ppermute x0 -> x42, waiting for transfers between devices: none -> 47.8 us  [the longest x14 29.8 us: line(): ends[s] = lax.ppermute(operand, 'in', pairs)]
    dot_general x6 -> x15, matrix products: 65.4 us -> 28.1 us  [the longest x10 17.8 us: line(): jnp.dot(packed[k], grad_basis[:, g * cut:(g + 1) * cut], preferred_elemen...]
    pallas_call x0 -> x5, Pallas kernels: none -> 22.5 us  [squares(): pl.pallas_call(body, grid=(1,), in_specs=specs, out_specs=pl.BlockSpec((c...]
    all_gather x1 -> x0, blocking collectives: 19.9 us -> none  [local(): lax.all_gather(activations, 'in', axis=1, tiled=True)]
    all_gather x2 -> x0, waiting for transfers between devices: 17.2 us -> none  [the longest x1 17.2 us: local(): lax.all_gather(gradients, 'out', axis=0, tiled=True)]
    div x1 -> x0, other arithmetic: 11.2 us -> none  [local(): return total / jnp.sum(weights)]
  transfers between devices with their start and end apart: 2 -> 42, of which waited for: 1 -> 10; matrix products, arithmetic and copies ran while one was open for 10% -> 24% of each run, Pallas kernels for 0% -> 0%
where the time goes in v1:
time: 185 us; the launch traced here: 184 us
  starting transfers between devices  67 us (36%)
  waiting for transfers between devices  47.8 us (26%)
  matrix products  28.1 us (15%)
  Pallas kernels  22.5 us (12%)
  local copies, waits for them, and re-layouts  10.2 us (6%)
  other arithmetic  7.66 us (4%)
    ppermute x14, starting transfers between devices, line(): ends[s] = lax.ppermute(operand, 'in', pairs)  41.7 us
    ppermute x14, waiting for transfers between devices, line(): ends[s] = lax.ppermute(operand, 'in', pairs)  29.8 us
    pallas_call x5, Pallas kernels, squares(): pl.pallas_call(body, grid=(1,), in_specs=specs, out_specs=pl.BlockSpec((c...  22.5 us
    dot_general x10, matrix products, line(): jnp.dot(packed[k], grad_basis[:, g * cut:(g + 1) * cut], preferred_elemen...  17.8 us
    ppermute x15, waiting for transfers between devices, swap(): return lax.ppermute(x, 'out', [(i, i ^ bit) for i in range(2 * seqs)])  13.1 us
    ppermute x15, starting transfers between devices, swap(): return lax.ppermute(x, 'out', [(i, i ^ bit) for i in range(2 * seqs)])  12.4 us
    dot_general x1, matrix products, line(): rot = jnp.dot(acts, act_basis, preferred_element_type=f32).astype(bf16)  7.08 us
    ppermute x10, starting transfers between devices, line(): mids[c] = lax.ppermute(own[c] + ends[c], 'in', middle)  6.91 us
  transfers between devices with their start and end apart: 42, of which 10 were waited for; matrix products, arithmetic and copies ran while one was open for 24% of the time, Pallas kernels for 0%

profile of v1, /device:TPU:0, one launch (start us, length us, event | category | flops | bytes accessed | tf_op | source)
XLA Modules:
  0.0 184.1 jit_solution(12342822244829544562)
XLA Ops:
  0.0 3.1 %collective-permute-start.24 = (bf16[64,1280]{1,0:T(8,128)(2,1)}, bf16[64,1280]{1,0:T(8,128)(2,1)}, u32[]{:S(2)}, u32[]{:S(2)}) collective-permute-start(bf16[64,1280]{1,0:T(8,128)(2,1)} %param.6), channel_id=1, source_target_pairs={{0,8},{8,16},{16,24},{24,0},{1,9},{9,17},{17,25},{25,1},{2,10},{10... | collective-permute-start | bytes 491528 | tf_op jit(solution)/shard_map/ppermute | solution.py:123
  3.1 2.0 %collective-permute-start.26 = (bf16[64,1280]{1,0:T(8,128)(2,1)}, bf16[64,1280]{1,0:T(8,128)(2,1)}, u32[]{:S(2)}, u32[]{:S(2)}) collective-permute-start(bf16[64,1280]{1,0:T(8,128)(2,1)} %param.6), channel_id=1, source_target_pairs={{0,24},{8,0},{16,8},{24,16},{1,25},{9,1},{17,9},{25,17},{2,26},{10... | collective-permute-start | bytes 491528 | tf_op jit(solution)/shard_map/ppermute | solution.py:123
  5.1 1.0 collective-permute-start.25
  6.1 1.9 %fusion.105 = (bf16[32,2560]{1,0:T(8,128)(2,1)S(1)}, bf16[512,2560]{1,0:T(8,128)(2,1)S(1)}, bf16[512,2560]{1,0:T(8,128)(2,1)}, bf16[32,2560]{1,0:T(8,128)(2,1)S(...) fusion(bf16[64,5120]{1,0:T(8,128)(2,1)} %param.8), kind=kLoop, calls=%fused_computation.261 | loop fusion | bytes 1638400 | tf_op jit(solution)/shard_map/slice | solution.py:116
  8.0 1.5 collective-permute-start.6
  9.5 1.5 collective-permute-start.9
  11.2 0.7 broadcast_subtract_fusion
  12.8 0.9 constant_dynamic-update-slice_fusion.18
  14.4 0.9 constant_dynamic-update-slice_fusion.17
  15.3 4.8 %collective-permute-done.25 = bf16[64,1280]{1,0:T(8,128)(2,1)} collective-permute-done((bf16[64,1280]{1,0:T(8,128)(2,1)}, bf16[64,1280]{1,0:T(8,128)(2,1)}, u32[]{:S(2)}, u32[]{:S(2)}) %collective-permute-start.25) | collective-permute-done | bytes 163872 | tf_op jit(solution)/shard_map/ppermute | solution.py:123
  20.1 1.5 collective-permute-start
  21.6 0.9 constant_dynamic-update-slice_fusion.16
  22.6 0.9 constant_dynamic-update-slice_fusion.19
  23.5 7.1 %convolution_convert_fusion.4 = bf16[64,1280]{1,0:T(8,128)(2,1)S(1)} fusion(bf16[64,5120]{1,0:T(8,128)(2,1)S(1)} %constant_dynamic-update-slice_fusion.19, bf16[5120,1280]{1,0:T(8,128)(2,1)} %param.7), kind=kOutput, calls=%fused_computation.24 | convolution fusion | flops 838942720 | bytes 13926400 | tf_op jit(solution)/shard_map/dot_general | solution.py:214
  31.2 1.1 pad_maximum_fusion.9
  32.3 1.6 collective-permute-start.7
  33.9 1.0 pad_maximum_fusion.10
  34.9 1.4 collective-permute-start.10
  36.3 0.8 collective-permute-start.4
  37.8 13.0 %collective-permute-done.4 = bf16[64,2560]{1,0:T(8,128)(2,1)S(1)} collective-permute-done((bf16[64,2560]{1,0:T(8,128)(2,1)S(1)}, bf16[64,2560]{1,0:T(8,128)(2,1)S(1)}, u32[]{:S(2)}, u32[]{:S(2)}) %collective-permute-start.4) | collective-permute-done | bytes 327712 | tf_op jit(solution)/shard_map/ppermute | solution.py:108
  51.5 1.0 pad_maximum_fusion.5
  52.7 1.0 pad_maximum_fusion.4
  54.3 1.1 constant_dynamic-update-slice_fusion.3
  55.4 1.2 constant_dynamic-update-slice_fusion.11
  57.1 1.4 convolution_convert_fusion.1
  58.4 4.7 %fusion.43 = f16[192,512]{1,0:T(8,128)(2,1)S(1)} fusion(bf16[5120,2560]{1,0:T(8,128)(2,1)} %param.9, bf16[192,2560]{1,0:T(8,128)(2,1)S(1)} %convolution_convert_fusion, bf16[192,2560]{1,0:T(8,128)(2,1)} %convolution_convert_fusion.1), kind=kOutput, calls=%fused_computation.44 | convolution fusion | flops 1010663424 | bytes 7405568 | tf_op jit(solution)/shard_map/dot_general | solution.py:181
  63.2 1.8 copy-done.3
  65.0 2.4 %fusion.61 = f16[192,512]{1,0:T(8,128)(2,1)S(1)} fusion(bf16[5120,2560]{1,0:T(8,128)(2,1)S(1)} %copy-done.3, bf16[192,2560]{1,0:T(8,128)(2,1)S(1)} %convolution_convert_fusion, bf16[192,2560]{1,0:T(8,128)(2,1)} %convolution_convert_fusion.1), kind=kOutput, calls=%fused_computation.50 | convolution fusion | flops 1010663424 | bytes 7405568 | tf_op jit(solution)/shard_map/dot_general | solution.py:181
  67.4 1.3 collective-permute-start.35
  68.7 1.3 collective-permute-start.30
  70.1 2.5 %fusion.52 = f16[192,512]{1,0:T(8,128)(2,1)S(1)} fusion(bf16[5120,2560]{1,0:T(8,128)(2,1)S(1)} %copy-done.3, bf16[192,2560]{1,0:T(8,128)(2,1)S(1)} %convolution_convert_fusion, bf16[192,2560]{1,0:T(8,128)(2,1)} %convolution_convert_fusion.1), kind=kOutput, calls=%fused_computation.47 | convolution fusion | flops 1010663424 | bytes 7405568 | tf_op jit(solution)/shard_map/dot_general | solution.py:181
  72.6 1.3 collective-permute-start.17
  74.0 1.2 fusion.46
  75.2 1.3 collective-permute-start.12
  77.2 8.7 %collective-permute-done.12 = f16[192,512]{1,0:T(8,128)(2,1)S(1)} collective-permute-done((f16[192,512]{1,0:T(8,128)(2,1)S(1)}, f16[192,512]{1,0:T(8,128)(2,1)S(1)}, u32[]{:S(2)}, u32[]{:S(2)}) %collective-permute-start.12) | collective-permute-done | bytes 196640 | tf_op jit(solution)/shard_map/ppermute | solution.py:197
  89.0 0.9 collective-permute-start.18
  89.9 1.2 add_select_fusion.5
  91.1 11.5 %collective-permute-start.14 = (f16[192,512]{1,0:T(8,128)(2,1)S(1)}, f16[192,512]{1,0:T(8,128)(2,1)S(1)}, u32[]{:S(2)}, u32[]{:S(2)}) collective-permute-start(f16[192,512]{1,0:T(8,128)(2,1)S(1)} %get-tuple-element.67), channel_id=1, source_target_pairs={{0,8},{24,16},{8,0},{16,24},{1,9},{25,17},{9,1},{17,25},{2,10},{26... | collective-permute-start | bytes 589832 | tf_op jit(solution)/shard_map/ppermute | solution.py:197
  102.6 1.2 add_select_fusion.3
  103.8 6.7 %collective-permute-start.19 = (f16[192,512]{1,0:T(8,128)(2,1)S(1)}, f16[192,512]{1,0:T(8,128)(2,1)S(1)}, u32[]{:S(2)}, u32[]{:S(2)}) collective-permute-start(f16[192,512]{1,0:T(8,128)(2,1)S(1)} %get-tuple-element.71), channel_id=1, source_target_pairs={{0,8},{24,16},{8,0},{16,24},{1,9},{25,17},{9,1},{17,25},{2,10},{26... | collective-permute-start | bytes 589832 | tf_op jit(solution)/shard_map/ppermute | solution.py:197
  110.5 1.2 add_select_fusion.1
  111.8 1.2 add_select_fusion
  113.0 2.1 %collective-permute-start.37 = (f16[192,512]{1,0:T(8,128)(2,1)S(1)}, f16[192,512]{1,0:T(8,128)(2,1)S(1)}, u32[]{:S(2)}, u32[]{:S(2)}) collective-permute-start(f16[192,512]{1,0:T(8,128)(2,1)S(1)} %get-tuple-element.77), channel_id=1, source_target_pairs={{0,8},{24,16},{8,0},{16,24},{1,9},{25,17},{9,1},{17,25},{2,10},{26... | collective-permute-start | bytes 589832 | tf_op jit(solution)/shard_map/ppermute | solution.py:197
  115.1 1.1 collective-permute-done.19
  116.9 1.0 collective-permute-start.28
  118.7 1.6 collective-permute-done.32
  121.1 2.0 %collective-permute-done.37 = f16[192,512]{1,0:T(8,128)(2,1)S(1)} collective-permute-done((f16[192,512]{1,0:T(8,128)(2,1)S(1)}, f16[192,512]{1,0:T(8,128)(2,1)S(1)}, u32[]{:S(2)}, u32[]{:S(2)}) %collective-permute-start.37) | collective-permute-done | bytes 196640 | tf_op jit(solution)/shard_map/ppermute | solution.py:197
  123.8 1.2 add_select_fusion.2
  125.0 7.9 %collective-permute-start.21 = (f16[192,512]{1,0:T(8,128)(2,1)S(1)}, f16[192,512]{1,0:T(8,128)(2,1)S(1)}, u32[]{:S(2)}, u32[]{:S(2)}) collective-permute-start(f16[192,512]{1,0:T(8,128)(2,1)S(1)} %get-tuple-element.73), channel_id=1, source_target_pairs={{0,8},{24,16},{8,0},{16,24},{1,9},{25,17},{9,1},{17,25},{2,10},{26... | collective-permute-start | bytes 589832 | tf_op jit(solution)/shard_map/ppermute | solution.py:197
  133.0 1.3 collective-permute-start.39
  134.3 1.2 add_select_fusion.4
  135.5 2.7 %collective-permute-start.16 = (f16[192,512]{1,0:T(8,128)(2,1)S(1)}, f16[192,512]{1,0:T(8,128)(2,1)S(1)}, u32[]{:S(2)}, u32[]{:S(2)}) collective-permute-start(f16[192,512]{1,0:T(8,128)(2,1)S(1)} %get-tuple-element.69), channel_id=1, source_target_pairs={{0,8},{24,16},{8,0},{16,24},{1,9},{25,17},{9,1},{17,25},{2,10},{26... | collective-permute-start | bytes 589832 | tf_op jit(solution)/shard_map/ppermute | solution.py:197
  138.5 1.3 collective-permute-start.41
  140.5 2.2 %collective-permute-done.16 = f16[192,512]{1,0:T(8,128)(2,1)S(1)} collective-permute-done((f16[192,512]{1,0:T(8,128)(2,1)S(1)}, f16[192,512]{1,0:T(8,128)(2,1)S(1)}, u32[]{:S(2)}, u32[]{:S(2)}) %collective-permute-start.16) | collective-permute-done | bytes 196640 | tf_op jit(solution)/shard_map/ppermute | solution.py:197
  143.7 1.3 collective-permute-start.23
  145.0 2.6 %collective-permute-done.41 = f16[192,512]{1,0:T(8,128)(2,1)S(1)} collective-permute-done((f16[192,512]{1,0:T(8,128)(2,1)S(1)}, f16[192,512]{1,0:T(8,128)(2,1)S(1)}, u32[]{:S(2)}, u32[]{:S(2)}) %collective-permute-start.41) | collective-permute-done | bytes 196640 | tf_op jit(solution)/shard_map/ppermute | solution.py:197
  147.9 1.5 collective-permute-start.34
  149.4 7.7 %collective-permute-done.23 = f16[192,512]{1,0:T(8,128)(2,1)S(1)} collective-permute-done((f16[192,512]{1,0:T(8,128)(2,1)S(1)}, f16[192,512]{1,0:T(8,128)(2,1)S(1)}, u32[]{:S(2)}, u32[]{:S(2)}) %collective-permute-start.23) | collective-permute-done | bytes 196640 | tf_op jit(solution)/shard_map/ppermute | solution.py:197
  157.4 3.9 %collective-permute-done.34 = f16[192,512]{1,0:T(8,128)(2,1)S(1)} collective-permute-done((f16[192,512]{1,0:T(8,128)(2,1)S(1)}, f16[192,512]{1,0:T(8,128)(2,1)S(1)}, u32[]{:S(2)}, u32[]{:S(2)}) %collective-permute-start.34) | collective-permute-done | bytes 196640 | tf_op jit(solution)/shard_map/ppermute | solution.py:197
  161.7 4.5 %shard_map.64.rest_4_ = f32[2560,1280]{1,0:T(8,128)} custom-call(s32[1]{0:T(128)} %bitcast.place_ref, s32[4]{0:T(128)S(1)} %copy-done, bf16[512,384]{1,0:T(8,128)(2,1)S(1)} %fusion.64.pick_ref, bf16[192,512]{1,0:T(8,128)(2,1)S(1)} %get-tuple-element.48.rest_0_, bf16[192,512]{1,0:T(8,128)(2,1)S(1)} %get-tuple-element.45.rest_1_, ...), custom_call_target="tpu_custom_call" | custom-call | flops 1342177280 | bytes 3932160 | tf_op jit(solution)/shard_map/pallas_call | solution.py:86
  166.2 4.5 %shard_map.65.rest_4_ = f32[2560,1280]{1,0:T(8,128)} custom-call(s32[1]{0:T(128)} %bitcast.place_ref, s32[4]{0:T(128)S(1)} %copy-done, bf16[512,384]{1,0:T(8,128)(2,1)S(1)} %fusion.64.pick_ref, bf16[192,512]{1,0:T(8,128)(2,1)S(1)} %get-tuple-element.46.rest_0_, bf16[192,512]{1,0:T(8,128)(2,1)S(1)} %get-tuple-element.51.rest_1_, ...), custom_call_target="tpu_custom_call", output_to_operand_aliasing={{}: (7, {})} | custom-call | flops 1342177280 | bytes 3932160 | tf_op jit(solution)/shard_map/pallas_call | solution.py:86
  170.7 4.5 %shard_map.66.rest_4_ = f32[2560,1280]{1,0:T(8,128)} custom-call(s32[1]{0:T(128)} %bitcast.place_ref, s32[4]{0:T(128)S(1)} %copy-done, bf16[512,384]{1,0:T(8,128)(2,1)S(1)} %fusion.64.pick_ref, bf16[192,512]{1,0:T(8,128)(2,1)S(1)} %get-tuple-element.52.rest_0_, bf16[192,512]{1,0:T(8,128)(2,1)S(1)} %get-tuple-element.53.rest_1_, ...), custom_call_target="tpu_custom_call", output_to_operand_aliasing={{}: (7, {})} | custom-call | flops 1342177280 | bytes 3932160 | tf_op jit(solution)/shard_map/pallas_call | solution.py:86
  175.1 4.5 %shard_map.67.rest_4_ = f32[2560,1280]{1,0:T(8,128)} custom-call(s32[1]{0:T(128)} %bitcast.place_ref, s32[4]{0:T(128)S(1)} %copy-done, bf16[512,384]{1,0:T(8,128)(2,1)S(1)} %fusion.64.pick_ref, bf16[192,512]{1,0:T(8,128)(2,1)S(1)} %get-tuple-element.54.rest_0_, bf16[192,512]{1,0:T(8,128)(2,1)S(1)} %get-tuple-element.50.rest_1_, ...), custom_call_target="tpu_custom_call", output_to_operand_aliasing={{}: (7, {})} | custom-call | flops 1342177280 | bytes 3932160 | tf_op jit(solution)/shard_map/pallas_call | solution.py:86
  179.6 4.5 %shard_map.68 = f32[2560,1280]{1,0:T(8,128)} custom-call(s32[1]{0:T(128)} %bitcast.place_ref, s32[4]{0:T(128)S(1)} %copy-done, bf16[512,384]{1,0:T(8,128)(2,1)S(1)} %fusion.64.pick_ref, bf16[192,512]{1,0:T(8,128)(2,1)S(1)} %get-tuple-element.49.rest_0_, bf16[192,512]{1,0:T(8,128)(2,1)S(1)} %get-tuple-element.47.rest_1_, ...), custom_call_target="tpu_custom_call", output_to_operand_aliasing={{}: (7, {})} | custom-call | flops 1342177280 | bytes 3932160 | tf_op jit(solution)/shard_map/pallas_call | solution.py:86
  (123 shorter events, 14.4 us)
Async XLA Ops:
  0.0 13.8 %collective-permute-start.24 = (bf16[64,1280]{1,0:T(8,128)(2,1)}, bf16[64,1280]{1,0:T(8,128)(2,1)}, u32[]{:S(2)}, u32[]{:S(2)}) collective-permute-start(bf16[64,1280]{1,0:T(8,128)(2,1)} %param.6), channel_id=1, source_target_pairs={{0,8},{8,16},{16,24},{24,0},{1,9},{9,17},{17,25},{25,1},{2,10},{10... | collective-permute-start | bytes 491528 | tf_op jit(solution)/shard_map/ppermute | solution.py:123
  3.1 19.5 %collective-permute-start.26 = (bf16[64,1280]{1,0:T(8,128)(2,1)}, bf16[64,1280]{1,0:T(8,128)(2,1)}, u32[]{:S(2)}, u32[]{:S(2)}) collective-permute-start(bf16[64,1280]{1,0:T(8,128)(2,1)} %param.6), channel_id=1, source_target_pairs={{0,24},{8,0},{16,8},{24,16},{1,25},{9,1},{17,9},{25,17},{2,26},{10... | collective-permute-start | bytes 491528 | tf_op jit(solution)/shard_map/ppermute | solution.py:123
  5.1 15.0 %collective-permute-start.25 = (bf16[64,1280]{1,0:T(8,128)(2,1)}, bf16[64,1280]{1,0:T(8,128)(2,1)}, u32[]{:S(2)}, u32[]{:S(2)}) collective-permute-start(bf16[64,1280]{1,0:T(8,128)(2,1)} %param.6), channel_id=1, source_target_pairs={{0,16},{8,24},{16,0},{24,8},{1,17},{9,25},{17,1},{25,9},{2,18},{10... | collective-permute-start | bytes 491528 | tf_op jit(solution)/shard_map/ppermute | solution.py:123
  8.0 23.2 %collective-permute-start.6 = (bf16[32,2560]{1,0:T(8,128)(2,1)S(1)}, bf16[32,2560]{1,0:T(8,128)(2,1)}, u32[]{:S(2)}, u32[]{:S(2)}) collective-permute-start(bf16[32,2560]{1,0:T(8,128)(2,1)S(1)} %get-tuple-element.37), channel_id=1, source_target_pairs={{0,2},{1,3},{2,0},{3,1},{4,6},{5,7},{6,4},{7,5},{8,10},{9,11},{10,... | collective-permute-start | bytes 491528 | tf_op jit(solution)/shard_map/ppermute | solution.py:108
  9.5 24.4 %collective-permute-start.9 = (bf16[32,2560]{1,0:T(8,128)(2,1)}, bf16[32,2560]{1,0:T(8,128)(2,1)}, u32[]{:S(2)}, u32[]{:S(2)}) collective-permute-start(bf16[32,2560]{1,0:T(8,128)(2,1)} %get-tuple-element.42), channel_id=1, source_target_pairs={{0,4},{1,5},{2,6},{3,7},{4,0},{5,1},{6,2},{7,3},{8,12},{9,13},{10,... | collective-permute-start | bytes 491528 | tf_op jit(solution)/shard_map/ppermute | solution.py:108
  13.8 22.5 %collective-permute-start.3 = (bf16[32,2560]{1,0:T(8,128)(2,1)S(1)}, bf16[32,2560]{1,0:T(8,128)(2,1)S(1)}, u32[]{:S(2)}, u32[]{:S(2)}) collective-permute-start(bf16[32,2560]{1,0:T(8,128)(2,1)S(1)} %get-tuple-element.40), channel_id=1, source_target_pairs={{0,4},{1,5},{2,6},{3,7},{4,0},{5,1},{6,2},{7,3},{8,12},{9,13},{10,... | collective-permute-start | bytes 491528 | tf_op jit(solution)/shard_map/ppermute | solution.py:108
  20.1 17.0 %collective-permute-start = (bf16[32,2560]{1,0:T(8,128)(2,1)S(1)}, bf16[32,2560]{1,0:T(8,128)(2,1)S(1)}, u32[]{:S(2)}, u32[]{:S(2)}) collective-permute-start(bf16[32,2560]{1,0:T(8,128)(2,1)S(1)} %get-tuple-element.41), channel_id=1, source_target_pairs={{0,2},{1,3},{2,0},{3,1},{4,6},{5,7},{6,4},{7,5},{8,10},{9,11},{10,... | collective-permute-start | bytes 491528 | tf_op jit(solution)/shard_map/ppermute | solution.py:108
  30.6 7.1 %copy-start.1 = (bf16[512,2560]{1,0:T(8,128)(2,1)S(1)}, bf16[512,2560]{1,0:T(8,128)(2,1)}, u32[]{:S(2)}) copy-start(bf16[512,2560]{1,0:T(8,128)(2,1)} %get-tuple-element.39) | copy-start | bytes 7864324
  30.6 86.3 %collective-permute-start.27 = (bf16[64,1280]{1,0:T(8,128)(2,1)S(1)}, bf16[64,1280]{1,0:T(8,128)(2,1)S(1)}, u32[]{:S(2)}, u32[]{:S(2)}) collective-permute-start(bf16[64,1280]{1,0:T(8,128)(2,1)S(1)} %convolution_convert_fusion.4), channel_id=1, source_target_pairs={{0,2},{1,3},{2,0},{3,1},{4,6},{5,7},{6,4},{7,5},{8,10},{9,11},{10,... | collective-permute-start | bytes 491528 | tf_op jit(solution)/shard_map/ppermute | solution.py:108
  32.3 20.4 %collective-permute-start.7 = (bf16[64,2560]{1,0:T(8,128)(2,1)S(1)}, bf16[64,2560]{1,0:T(8,128)(2,1)S(1)}, u32[]{:S(2)}, u32[]{:S(2)}) collective-permute-start(bf16[64,2560]{1,0:T(8,128)(2,1)S(1)} %pad_maximum_fusion.9), channel_id=1, source_target_pairs={{0,4},{1,5},{2,6},{3,7},{4,0},{5,1},{6,2},{7,3},{8,12},{9,13},{10,... | collective-permute-start | bytes 983048 | tf_op jit(solution)/shard_map/ppermute | solution.py:108
  34.9 16.6 %collective-permute-start.10 = (bf16[64,2560]{1,0:T(8,128)(2,1)S(1)}, bf16[64,2560]{1,0:T(8,128)(2,1)S(1)}, u32[]{:S(2)}, u32[]{:S(2)}) collective-permute-start(bf16[64,2560]{1,0:T(8,128)(2,1)S(1)} %pad_maximum_fusion.10), channel_id=1, source_target_pairs={{0,2},{1,3},{2,0},{3,1},{4,6},{5,7},{6,4},{7,5},{8,10},{9,11},{10,... | collective-permute-start | bytes 983048 | tf_op jit(solution)/shard_map/ppermute | solution.py:108
  36.3 14.5 %collective-permute-start.4 = (bf16[64,2560]{1,0:T(8,128)(2,1)S(1)}, bf16[64,2560]{1,0:T(8,128)(2,1)S(1)}, u32[]{:S(2)}, u32[]{:S(2)}) collective-permute-start(bf16[64,2560]{1,0:T(8,128)(2,1)S(1)} %pad_maximum_fusion.8), channel_id=1, source_target_pairs={{0,2},{1,3},{2,0},{3,1},{4,6},{5,7},{6,4},{7,5},{8,10},{9,11},{10,... | collective-permute-start | bytes 983048 | tf_op jit(solution)/shard_map/ppermute | solution.py:108
  37.1 13.8 %collective-permute-start.1 = (bf16[64,2560]{1,0:T(8,128)(2,1)S(1)}, bf16[64,2560]{1,0:T(8,128)(2,1)S(1)}, u32[]{:S(2)}, u32[]{:S(2)}) collective-permute-start(bf16[64,2560]{1,0:T(8,128)(2,1)S(1)} %pad_maximum_fusion.7), channel_id=1, source_target_pairs={{0,4},{1,5},{2,6},{3,7},{4,0},{5,1},{6,2},{7,3},{8,12},{9,13},{10,... | collective-permute-start | bytes 983048 | tf_op jit(solution)/shard_map/ppermute | solution.py:108
  50.8 3.4 %copy-start.2 = (bf16[64,5120]{1,0:T(8,128)(2,1)S(1)}, bf16[64,5120]{1,0:T(8,128)(2,1)}, u32[]{:S(2)}) copy-start(bf16[64,5120]{1,0:T(8,128)(2,1)} %param.8) | copy-start | bytes 1966084
  50.8 5.8 %collective-permute-start.5 = (bf16[128,2560]{1,0:T(8,128)(2,1)S(1)}, bf16[128,2560]{1,0:T(8,128)(2,1)S(1)}, u32[]{:S(2)}, u32[]{:S(2)}) collective-permute-start(bf16[128,2560]{1,0:T(8,128)(2,1)S(1)} %pad_maximum_fusion.3), channel_id=1, source_target_pairs={{0,1},{1,0},{2,3},{3,2},{4,5},{5,4},{6,7},{7,6},{8,9},{9,8},{10,11... | collective-permute-start | bytes 1966088 | tf_op jit(solution)/shard_map/ppermute | solution.py:108
  51.0 6.1 %collective-permute-start.2 = (bf16[128,2560]{1,0:T(8,128)(2,1)S(1)}, bf16[128,2560]{1,0:T(8,128)(2,1)S(1)}, u32[]{:S(2)}, u32[]{:S(2)}) collective-permute-start(bf16[128,2560]{1,0:T(8,128)(2,1)S(1)} %pad_maximum_fusion.2), channel_id=1, source_target_pairs={{0,1},{1,0},{2,3},{3,2},{4,5},{5,4},{6,7},{7,6},{8,9},{9,8},{10,11... | collective-permute-start | bytes 1966088 | tf_op jit(solution)/shard_map/ppermute | solution.py:108
  52.6 20.0 %collective-permute-start.11 = (bf16[128,2560]{1,0:T(8,128)(2,1)S(1)}, bf16[128,2560]{1,0:T(8,128)(2,1)S(1)}, u32[]{:S(2)}, u32[]{:S(2)}) collective-permute-start(bf16[128,2560]{1,0:T(8,128)(2,1)S(1)} %pad_maximum_fusion.5), channel_id=1, source_target_pairs={{0,1},{1,0},{2,3},{3,2},{4,5},{5,4},{6,7},{7,6},{8,9},{9,8},{10,11... | collective-permute-start | bytes 1966088 | tf_op jit(solution)/shard_map/ppermute | solution.py:108
  53.6 21.5 %collective-permute-start.8 = (bf16[128,2560]{1,0:T(8,128)(2,1)S(1)}, bf16[128,2560]{1,0:T(8,128)(2,1)S(1)}, u32[]{:S(2)}, u32[]{:S(2)}) collective-permute-start(bf16[128,2560]{1,0:T(8,128)(2,1)S(1)} %pad_maximum_fusion.4), channel_id=1, source_target_pairs={{0,1},{1,0},{2,3},{3,2},{4,5},{5,4},{6,7},{7,6},{8,9},{9,8},{10,11... | collective-permute-start | bytes 1966088 | tf_op jit(solution)/shard_map/ppermute | solution.py:108
  54.2 10.8 %copy-start.3 = (bf16[5120,2560]{1,0:T(8,128)(2,1)S(1)}, bf16[5120,2560]{1,0:T(8,128)(2,1)}, u32[]{:S(2)}) copy-start(bf16[5120,2560]{1,0:T(8,128)(2,1)} %param.9) | copy-start | bytes 78643200
  67.4 20.0 %collective-permute-start.35 = (f16[192,512]{1,0:T(8,128)(2,1)S(1)}, f16[192,512]{1,0:T(8,128)(2,1)S(1)}, u32[]{:S(2)}, u32[]{:S(2)}) collective-permute-start(f16[192,512]{1,0:T(8,128)(2,1)S(1)} %fusion.61), channel_id=1, source_target_pairs={{0,8},{24,16},{1,9},{25,17},{2,10},{26,18},{3,11},{27,19},{4,12},{... | collective-permute-start | bytes 589832 | tf_op jit(solution)/shard_map/ppermute | solution.py:197
  68.7 19.5 %collective-permute-start.30 = (f16[192,512]{1,0:T(8,128)(2,1)S(1)}, f16[192,512]{1,0:T(8,128)(2,1)S(1)}, u32[]{:S(2)}, u32[]{:S(2)}) collective-permute-start(f16[192,512]{1,0:T(8,128)(2,1)S(1)} %fusion.43), channel_id=1, source_target_pairs={{0,8},{24,16},{1,9},{25,17},{2,10},{26,18},{3,11},{27,19},{4,12},{... | collective-permute-start | bytes 589832 | tf_op jit(solution)/shard_map/ppermute | solution.py:197
  70.1 3.9 %copy-start.4 = (bf16[192,2560]{1,0:T(8,128)(2,1)S(1)}, bf16[192,2560]{1,0:T(8,128)(2,1)}, u32[]{:S(2)}) copy-start(bf16[192,2560]{1,0:T(8,128)(2,1)} %convolution_convert_fusion.1) | copy-start | bytes 2949124
  72.6 16.3 %collective-permute-start.17 = (f16[192,512]{1,0:T(8,128)(2,1)S(1)}, f16[192,512]{1,0:T(8,128)(2,1)S(1)}, u32[]{:S(2)}, u32[]{:S(2)}) collective-permute-start(f16[192,512]{1,0:T(8,128)(2,1)S(1)} %fusion.52), channel_id=1, source_target_pairs={{0,8},{24,16},{1,9},{25,17},{2,10},{26,18},{3,11},{27,19},{4,12},{... | collective-permute-start | bytes 589832 | tf_op jit(solution)/shard_map/ppermute | solution.py:197
  75.2 10.8 %collective-permute-start.12 = (f16[192,512]{1,0:T(8,128)(2,1)S(1)}, f16[192,512]{1,0:T(8,128)(2,1)S(1)}, u32[]{:S(2)}, u32[]{:S(2)}) collective-permute-start(f16[192,512]{1,0:T(8,128)(2,1)S(1)} %fusion.46), channel_id=1, source_target_pairs={{0,8},{24,16},{1,9},{25,17},{2,10},{26,18},{3,11},{27,19},{4,12},{... | collective-permute-start | bytes 589832 | tf_op jit(solution)/shard_map/ppermute | solution.py:197
  86.0 3.9 %collective-permute-start.13 = (f16[192,512]{1,0:T(8,128)(2,1)S(1)}, f16[192,512]{1,0:T(8,128)(2,1)S(1)}, u32[]{:S(2)}, u32[]{:S(2)}) collective-permute-start(f16[192,512]{1,0:T(8,128)(2,1)S(1)} %add.752), channel_id=1, source_target_pairs={{8,16},{16,8},{9,17},{17,9},{10,18},{18,10},{11,19},{19,11},{12,20... | collective-permute-start | bytes 589832 | tf_op jit(solution)/shard_map/ppermute | solution.py:200
  86.7 3.2 %copy-start.5 = (bf16[192,2560]{1,0:T(8,128)(2,1)S(1)}, bf16[192,2560]{1,0:T(8,128)(2,1)}, u32[]{:S(2)}) copy-start(bf16[192,2560]{1,0:T(8,128)(2,1)} %convolution_convert_fusion.1) | copy-start | bytes 2949124
  87.5 24.3 %collective-permute-start.36 = (f16[192,512]{1,0:T(8,128)(2,1)S(1)}, f16[192,512]{1,0:T(8,128)(2,1)S(1)}, u32[]{:S(2)}, u32[]{:S(2)}) collective-permute-start(f16[192,512]{1,0:T(8,128)(2,1)S(1)} %add.779), channel_id=1, source_target_pairs={{8,16},{16,8},{9,17},{17,9},{10,18},{18,10},{11,19},{19,11},{12,20... | collective-permute-start | bytes 589832 | tf_op jit(solution)/shard_map/ppermute | solution.py:200
  88.2 22.3 %collective-permute-start.31 = (f16[192,512]{1,0:T(8,128)(2,1)S(1)}, f16[192,512]{1,0:T(8,128)(2,1)S(1)}, u32[]{:S(2)}, u32[]{:S(2)}) collective-permute-start(f16[192,512]{1,0:T(8,128)(2,1)S(1)} %add.771), channel_id=1, source_target_pairs={{8,16},{16,8},{9,17},{17,9},{10,18},{18,10},{11,19},{19,11},{12,20... | collective-permute-start | bytes 589832 | tf_op jit(solution)/shard_map/ppermute | solution.py:200
  89.0 13.6 %collective-permute-start.18 = (f16[192,512]{1,0:T(8,128)(2,1)S(1)}, f16[192,512]{1,0:T(8,128)(2,1)S(1)}, u32[]{:S(2)}, u32[]{:S(2)}) collective-permute-start(f16[192,512]{1,0:T(8,128)(2,1)S(1)} %add.758), channel_id=1, source_target_pairs={{8,16},{16,8},{9,17},{17,9},{10,18},{18,10},{11,19},{19,11},{12,20... | collective-permute-start | bytes 589832 | tf_op jit(solution)/shard_map/ppermute | solution.py:200
  91.1 26.9 %collective-permute-start.14 = (f16[192,512]{1,0:T(8,128)(2,1)S(1)}, f16[192,512]{1,0:T(8,128)(2,1)S(1)}, u32[]{:S(2)}, u32[]{:S(2)}) collective-permute-start(f16[192,512]{1,0:T(8,128)(2,1)S(1)} %get-tuple-element.67), channel_id=1, source_target_pairs={{0,8},{24,16},{8,0},{16,24},{1,9},{25,17},{9,1},{17,25},{2,10},{26... | collective-permute-start | bytes 589832 | tf_op jit(solution)/shard_map/ppermute | solution.py:197
  103.8 12.3 %collective-permute-start.19 = (f16[192,512]{1,0:T(8,128)(2,1)S(1)}, f16[192,512]{1,0:T(8,128)(2,1)S(1)}, u32[]{:S(2)}, u32[]{:S(2)}) collective-permute-start(f16[192,512]{1,0:T(8,128)(2,1)S(1)} %get-tuple-element.71), channel_id=1, source_target_pairs={{0,8},{24,16},{8,0},{16,24},{1,9},{25,17},{9,1},{17,25},{2,10},{26... | collective-permute-start | bytes 589832 | tf_op jit(solution)/shard_map/ppermute | solution.py:197
  111.7 8.6 %collective-permute-start.32 = (f16[192,512]{1,0:T(8,128)(2,1)S(1)}, f16[192,512]{1,0:T(8,128)(2,1)S(1)}, u32[]{:S(2)}, u32[]{:S(2)}) collective-permute-start(f16[192,512]{1,0:T(8,128)(2,1)S(1)} %get-tuple-element.75), channel_id=1, source_target_pairs={{0,8},{24,16},{8,0},{16,24},{1,9},{25,17},{9,1},{17,25},{2,10},{26... | collective-permute-start | bytes 589832 | tf_op jit(solution)/shard_map/ppermute | solution.py:197
  113.0 10.1 %collective-permute-start.37 = (f16[192,512]{1,0:T(8,128)(2,1)S(1)}, f16[192,512]{1,0:T(8,128)(2,1)S(1)}, u32[]{:S(2)}, u32[]{:S(2)}) collective-permute-start(f16[192,512]{1,0:T(8,128)(2,1)S(1)} %get-tuple-element.77), channel_id=1, source_target_pairs={{0,8},{24,16},{8,0},{16,24},{1,9},{25,17},{9,1},{17,25},{2,10},{26... | collective-permute-start | bytes 589832 | tf_op jit(solution)/shard_map/ppermute | solution.py:197
  116.2 7.6 %collective-permute-start.20 = (f16[192,512]{1,0:T(8,128)(2,1)S(1)}, f16[192,512]{1,0:T(8,128)(2,1)S(1)}, u32[]{:S(2)}, u32[]{:S(2)}) collective-permute-start(f16[192,512]{1,0:T(8,128)(2,1)S(1)} %add.760), channel_id=1, source_target_pairs={{8,16},{16,8},{9,17},{17,9},{10,18},{18,10},{11,19},{19,11},{12,20... | collective-permute-start | bytes 589832 | tf_op jit(solution)/shard_map/ppermute | solution.py:200
  116.9 21.3 %collective-permute-start.28 = (bf16[128,1280]{1,0:T(8,128)(2,1)S(1)}, bf16[128,1280]{1,0:T(8,128)(2,1)S(1)}, u32[]{:S(2)}, u32[]{:S(2)}) collective-permute-start(bf16[128,1280]{1,0:T(8,128)(2,1)S(1)} %pad_maximum_fusion.11), channel_id=1, source_target_pairs={{0,4},{1,5},{2,6},{3,7},{4,0},{5,1},{6,2},{7,3},{8,12},{9,13},{10,... | collective-permute-start | bytes 983048 | tf_op jit(solution)/shard_map/ppermute | solution.py:108
  118.0 16.3 %collective-permute-start.15 = (f16[192,512]{1,0:T(8,128)(2,1)S(1)}, f16[192,512]{1,0:T(8,128)(2,1)S(1)}, u32[]{:S(2)}, u32[]{:S(2)}) collective-permute-start(f16[192,512]{1,0:T(8,128)(2,1)S(1)} %add.754), channel_id=1, source_target_pairs={{8,16},{16,8},{9,17},{17,9},{10,18},{18,10},{11,19},{19,11},{12,20... | collective-permute-start | bytes 589832 | tf_op jit(solution)/shard_map/ppermute | solution.py:200
  120.4 12.6 %collective-permute-start.38 = (f16[192,512]{1,0:T(8,128)(2,1)S(1)}, f16[192,512]{1,0:T(8,128)(2,1)S(1)}, u32[]{:S(2)}, u32[]{:S(2)}) collective-permute-start(f16[192,512]{1,0:T(8,128)(2,1)S(1)} %add.783), channel_id=1, source_target_pairs={{8,16},{16,8},{9,17},{17,9},{10,18},{18,10},{11,19},{19,11},{12,20... | collective-permute-start | bytes 589832 | tf_op jit(solution)/shard_map/ppermute | solution.py:200
  123.1 15.3 %collective-permute-start.40 = (f16[192,512]{1,0:T(8,128)(2,1)S(1)}, f16[192,512]{1,0:T(8,128)(2,1)S(1)}, u32[]{:S(2)}, u32[]{:S(2)}) collective-permute-start(f16[192,512]{1,0:T(8,128)(2,1)S(1)} %add.789), channel_id=1, source_target_pairs={{8,16},{16,8},{9,17},{17,9},{10,18},{18,10},{11,19},{19,11},{12,20... | collective-permute-start | bytes 589832 | tf_op jit(solution)/shard_map/ppermute | solution.py:200
  125.0 14.7 %collective-permute-start.21 = (f16[192,512]{1,0:T(8,128)(2,1)S(1)}, f16[192,512]{1,0:T(8,128)(2,1)S(1)}, u32[]{:S(2)}, u32[]{:S(2)}) collective-permute-start(f16[192,512]{1,0:T(8,128)(2,1)S(1)} %get-tuple-element.73), channel_id=1, source_target_pairs={{0,8},{24,16},{8,0},{16,24},{1,9},{25,17},{9,1},{17,25},{2,10},{26... | collective-permute-start | bytes 589832 | tf_op jit(solution)/shard_map/ppermute | solution.py:197
  133.0 10.4 %collective-permute-start.39 = (f16[192,512]{1,0:T(8,128)(2,1)S(1)}, f16[192,512]{1,0:T(8,128)(2,1)S(1)}, u32[]{:S(2)}, u32[]{:S(2)}) collective-permute-start(f16[192,512]{1,0:T(8,128)(2,1)S(1)} %add.784), channel_id=1, source_target_pairs={{8,0},{16,24},{9,1},{17,25},{10,2},{18,26},{11,3},{19,27},{12,4},{... | collective-permute-start | bytes 589832 | tf_op jit(solution)/shard_map/ppermute | solution.py:197
  135.5 7.2 %collective-permute-start.16 = (f16[192,512]{1,0:T(8,128)(2,1)S(1)}, f16[192,512]{1,0:T(8,128)(2,1)S(1)}, u32[]{:S(2)}, u32[]{:S(2)}) collective-permute-start(f16[192,512]{1,0:T(8,128)(2,1)S(1)} %get-tuple-element.69), channel_id=1, source_target_pairs={{0,8},{24,16},{8,0},{16,24},{1,9},{25,17},{9,1},{17,25},{2,10},{26... | collective-permute-start | bytes 589832 | tf_op jit(solution)/shard_map/ppermute | solution.py:197
  138.3 23.4 %collective-permute-start.29 = (bf16[256,1280]{1,0:T(8,128)(2,1)S(1)}, bf16[256,1280]{1,0:T(8,128)(2,1)S(1)}, u32[]{:S(2)}, u32[]{:S(2)}) collective-permute-start(bf16[256,1280]{1,0:T(8,128)(2,1)S(1)} %pad_maximum_fusion.6.rest_2_), channel_id=1, source_target_pairs={{0,1},{1,0},{2,3},{3,2},{4,5},{5,4},{6,7},{7,6},{8,9},{9,8},{10,11... | collective-permute-start | bytes 1966088 | tf_op jit(solution)/shard_map/ppermute | solution.py:108
  138.5 9.2 %collective-permute-start.41 = (f16[192,512]{1,0:T(8,128)(2,1)S(1)}, f16[192,512]{1,0:T(8,128)(2,1)S(1)}, u32[]{:S(2)}, u32[]{:S(2)}) collective-permute-start(f16[192,512]{1,0:T(8,128)(2,1)S(1)} %add.790), channel_id=1, source_target_pairs={{8,0},{16,24},{9,1},{17,25},{10,2},{18,26},{11,3},{19,27},{12,4},{... | collective-permute-start | bytes 589832 | tf_op jit(solution)/shard_map/ppermute | solution.py:197
  139.8 3.8 %collective-permute-start.22 = (f16[192,512]{1,0:T(8,128)(2,1)S(1)}, f16[192,512]{1,0:T(8,128)(2,1)S(1)}, u32[]{:S(2)}, u32[]{:S(2)}) collective-permute-start(f16[192,512]{1,0:T(8,128)(2,1)S(1)} %add.762), channel_id=1, source_target_pairs={{8,16},{16,8},{9,17},{17,9},{10,18},{18,10},{11,19},{19,11},{12,20... | collective-permute-start | bytes 589832 | tf_op jit(solution)/shard_map/ppermute | solution.py:200
  142.8 5.1 %collective-permute-start.33 = (f16[192,512]{1,0:T(8,128)(2,1)S(1)}, f16[192,512]{1,0:T(8,128)(2,1)S(1)}, u32[]{:S(2)}, u32[]{:S(2)}) collective-permute-start(f16[192,512]{1,0:T(8,128)(2,1)S(1)} %add.775), channel_id=1, source_target_pairs={{8,16},{16,8},{9,17},{17,9},{10,18},{18,10},{11,19},{19,11},{12,20... | collective-permute-start | bytes 589832 | tf_op jit(solution)/shard_map/ppermute | solution.py:200
  143.7 13.4 %collective-permute-start.23 = (f16[192,512]{1,0:T(8,128)(2,1)S(1)}, f16[192,512]{1,0:T(8,128)(2,1)S(1)}, u32[]{:S(2)}, u32[]{:S(2)}) collective-permute-start(f16[192,512]{1,0:T(8,128)(2,1)S(1)} %add.763), channel_id=1, source_target_pairs={{8,0},{16,24},{9,1},{17,25},{10,2},{18,26},{11,3},{19,27},{12,4},{... | collective-permute-start | bytes 589832 | tf_op jit(solution)/shard_map/ppermute | solution.py:197
  147.9 13.7 %copy-start = (s32[4]{0:T(128)S(1)}, s32[4]{0:T(128)}, u32[]{:S(2)}) copy-start(s32[4]{0:T(128)} %weight_ref.9) | copy-start | bytes 52
  147.9 13.4 %collective-permute-start.34 = (f16[192,512]{1,0:T(8,128)(2,1)S(1)}, f16[192,512]{1,0:T(8,128)(2,1)S(1)}, u32[]{:S(2)}, u32[]{:S(2)}) collective-permute-start(f16[192,512]{1,0:T(8,128)(2,1)S(1)} %add.776), channel_id=1, source_target_pairs={{8,0},{16,24},{9,1},{17,25},{10,2},{18,26},{11,3},{19,27},{12,4},{... | collective-permute-start | bytes 589832 | tf_op jit(solution)/shard_map/ppermute | solution.py:197
